TPU v7x, 32 devices: a whole 2x2x4 slice. The times are simulated.
32 devices in a mesh: ctx: 4 (over y, core), head: 2 (over x), dp: 4 (over z).
Axes of the slice: x: 2, y: 2, z: 4, core: 2. Of those that a mesh axis runs over, the one named last changes fastest.
Arguments:
- queries: bfloat16 [1024, 6144], P(('dp', 'ctx', 'head')), parts along dimension 0, may hold values from -18 to 18
- keys: bfloat16 [1024, 1024], P(('dp', 'ctx', 'head')), parts along dimension 0, may hold values from -9 to 9
- values: bfloat16 [1024, 1024], P(('dp', 'ctx', 'head')), parts along dimension 0, may hold values from -6 to 6
- level_gain: float32 [64, 6144], P(None, 'head'), may hold values from 0.5 to 4
- levels: int32 [16], P('dp'), parts along dimension 0, may hold values from 0 to 63
- visible: int32 [16, 4], P('dp'), parts along dimension 0, may hold values from 0 to 1, as said below
- counts: int32 [16], P('dp'), parts along dimension 0, may hold values from 32 to 64, as said below
Outputs:
- mixed: bfloat16 [1024, 6144], P(('dp', 'ctx', 'head')), parts along dimension 0
- finished: bfloat16 [256, 6144], P(('dp', 'ctx'), 'head'), parts along dimension 0
There are 4 independent parts, one for each index of `dp`. A program takes and returns all parts, laid end to end along the dimension named above; an argument that names none is the same for every part. Nothing has to cross between parts.
Inputs may be any that keep to these rules, and one draw needn't show every extreme that they name: visible[c][c] is 1, visible[c][d] is 0 for d > c, and entries below the diagonal are 0 or 1. `counts`: every clip has at least half of its slots live, and in every draw some clip has all 64 live.
All inputs are finite; a program needn't handle non-finite values.
Results may differ from a plain program's by a relative error of at most 0.0045.
Values may be sent and summed in bfloat16 or wider, within the bound.
No kernel may reach another device: no remote copies, remote signals or barrier semaphores. Data moves between devices by JAX's collectives and lax.ppermute only.
A program may use at most 64 MiB of HBM per device.

v0:
```python
import math
import jax
import jax.numpy as jnp
from jax import lax
from jax.sharding import PartitionSpec as P

QUERY_HEADS = 48
KEY_VALUE_HEADS = 8
HEAD_SIZE = 128
LEVELS = 64
CLIPS = 4


def from_behind(block, axis, distance):
    devices = range(lax.axis_size(axis))
    route = [(i - distance, i) for i in devices if i - distance in devices]
    return lax.ppermute(block, axis, route)


def body(queries, keys, values, level_gain, levels, visible, counts):
    head_count = lax.axis_size("head")
    ctx_count = lax.axis_size("ctx")
    ctx_index = lax.axis_index("ctx")
    tok_rows = queries.shape[0]
    rows_ctx = tok_rows * head_count
    clip_tok = rows_ctx * ctx_count // CLIPS
    heads_per_group = QUERY_HEADS // KEY_VALUE_HEADS
    scale = 1.0 / math.sqrt(HEAD_SIZE)
    clip_range = jnp.arange(CLIPS, dtype=jnp.int32)
    source_count = ctx_count // CLIPS
    query_local, key_local, value_local = (
        lax.all_to_all(queries, "head", split_axis=1, concat_axis=0, tiled=True),
        lax.all_to_all(keys, "head", split_axis=1, concat_axis=0, tiled=True),
        lax.all_to_all(values, "head", split_axis=1, concat_axis=0, tiled=True),
    )
    query_width = query_local.shape[1]
    query_ids = ctx_index * rows_ctx + jnp.arange(rows_ctx, dtype=jnp.int32)
    row_groups = [(0, rows_ctx)]
    query_grouped = query_local.reshape(rows_ctx, -1, heads_per_group, HEAD_SIZE)
    local_kv_heads = query_grouped.shape[1]
    query_onehot = (query_ids // clip_tok)[:, None] == clip_range[None, :]
    query_count = jnp.sum(jnp.where(query_onehot, counts[None, :], 0), axis=1)
    query_live = query_ids % clip_tok < query_count
    query_sees = jnp.sum(jnp.where(query_onehot[:, :, None], visible[None, :, :], 0), axis=1) == 1
    query_level = jnp.sum(jnp.where(query_onehot, levels[None, :], 0), axis=1)

    def key_block(carry_state, key_block_rows, value_block_rows, first_row):
        block_rows = key_block_rows.shape[0]
        key_ids = first_row + jnp.arange(block_rows, dtype=jnp.int32)
        key_onehot = (key_ids // clip_tok)[:, None] == clip_range[None, :]
        key_count = jnp.sum(jnp.where(key_onehot, counts[None, :], 0), axis=1)
        key_live = key_ids % clip_tok < key_count
        block_clips = jnp.any(key_onehot & key_live[:, None], axis=0)
        key_head_rows = key_block_rows.reshape(block_rows, -1, HEAD_SIZE)
        value_head_rows = value_block_rows.reshape(block_rows, -1, HEAD_SIZE)
        group_start, group_rows = row_groups[0]
        group_end = group_start + group_rows
        part_state = tuple((member for member in carry_state))
        group_sees = query_sees
        needed = jnp.any(jnp.any(group_sees, axis=0) & block_clips)

        def update(state, group_sees=group_sees, group_start=group_start, group_end=group_end):
            running_max, denominator, weighted = state
            allowed = (
                jnp.any(group_sees[:, None, :] & key_onehot[None, :, :], axis=-1)
                & key_live[None, :]
            )
            scores = (
                jnp.einsum(
                    "rkgd,nkd->rkgn",
                    query_grouped,
                    key_head_rows,
                    preferred_element_type=jnp.float32,
                )
                * scale
            )
            key_mask = allowed[:, None, None, :]
            scores = jnp.where(key_mask, scores, -1e30)
            new_max = jnp.maximum(running_max, jnp.max(scores, axis=-1))
            weights = jnp.where(key_mask, jnp.exp(scores - new_max[..., None]), 0.0)
            shrink = jnp.exp(running_max - new_max)
            denominator = denominator * shrink + jnp.sum(weights, axis=-1)
            weighted = weighted * shrink[..., None] + jnp.einsum(
                "rkgn,nkd->rkgd",
                weights.astype(jnp.bfloat16),
                value_head_rows,
                preferred_element_type=jnp.float32,
            )
            return (new_max, denominator, weighted)

        def keep(state):
            return state

        group_states = [lax.cond(needed, update, keep, part_state)]
        if len(group_states) == 1:
            return group_states[0]
        return tuple(
            (
                jnp.concatenate([state[member] for state in group_states], axis=0)
                for member in range(3)
            )
        )

    initial = (
        jnp.full((rows_ctx, local_kv_heads, heads_per_group), -1e30, jnp.float32),
        jnp.zeros((rows_ctx, local_kv_heads, heads_per_group), jnp.float32),
        jnp.zeros((rows_ctx, local_kv_heads, heads_per_group, HEAD_SIZE), jnp.float32),
    )
    key_piece = lax.all_gather(key_local, "ctx", axis=0, tiled=True)
    value_piece = lax.all_gather(value_local, "ctx", axis=0, tiled=True)
    piece_rows = key_piece.shape[0]
    block_rows = math.gcd(piece_rows, 512)

    def advance(block_index, inner_state):
        key_slice = lax.dynamic_slice_in_dim(key_piece, block_index * block_rows, block_rows, 0)
        value_slice = lax.dynamic_slice_in_dim(value_piece, block_index * block_rows, block_rows, 0)
        return key_block(inner_state, key_slice, value_slice, block_index * block_rows)

    final_state = lax.fori_loop(0, piece_rows // block_rows, advance, initial)
    attended = (final_state[2] / final_state[1][..., None]).reshape(rows_ctx, query_width)
    level_onehot = (query_level[:, None] == jnp.arange(LEVELS, dtype=jnp.int32)[None, :]).astype(
        jnp.float32
    )
    gate_rows = jnp.dot(
        level_onehot,
        level_gain,
        precision=lax.Precision.HIGHEST,
        preferred_element_type=jnp.float32,
    )
    gated = jnp.where(query_live[:, None], attended * gate_rows, 0.0).astype(jnp.bfloat16)
    mixed = lax.all_to_all(gated, "head", split_axis=0, concat_axis=1, tiled=True)
    relay_rows = rows_ctx // CLIPS
    held = jnp.where(ctx_index < source_count, gated, jnp.zeros_like(gated)).reshape(
        CLIPS, relay_rows, query_width
    )
    empty_block = jnp.zeros_like(held)
    sources = jnp.arange(source_count, dtype=jnp.int32)
    hop_bits = (source_count - 1).bit_length()
    for bit_number in reversed(range(hop_bits)):
        higher = sources >> bit_number + 1 << bit_number + 1
        places = sources + 3 * higher
        holds_bit = jnp.any((places == ctx_index) & (sources >> bit_number & 1 == 1))
        moving = jnp.where(holds_bit, held, empty_block)
        staying = jnp.where(holds_bit, empty_block, held)
        arriving = from_behind(moving, "ctx", 3 * (1 << bit_number))
        held = staying + arriving
    group_position = ctx_index % CLIPS
    finished = held[0]
    for lane_number in range(1, CLIPS):
        arriving_tile = from_behind(held[lane_number], "ctx", lane_number)
        finished = jnp.where(group_position == lane_number, arriving_tile, finished)
    return (mixed, finished)


def solution(mesh):
    placed = (
        P(("dp", "ctx", "head"), None),
        P(("dp", "ctx", "head"), None),
        P(("dp", "ctx", "head"), None),
        P(None, "head"),
        P("dp"),
        P("dp", None),
        P("dp"),
    )
    return jax.shard_map(
        body,
        mesh=mesh,
        in_specs=placed,
        out_specs=(P(("dp", "ctx", "head"), None), P(("dp", "ctx"), "head")),
        check_vma=False,
    )
```

profile of v0, /device:TPU:0, one launch (start us, length us, event | category | flops | bytes accessed | tf_op | source)
XLA Modules:
  0.0 61.5 jit_solution(9454937511669953927)
XLA Ops:
  0.6 1.5 %copy.71 = bf16[4,2,8,512]{3,2,0,1:T(8,128)(2,1)} copy(bf16[4,2,8,512]{3,2,1,0:T(8,128)(2,1)} %bitcast.40) | data formatting | bytes 131072 | tf_op jit(solution)/shard_map/all_to_all | solution.py:33
  2.2 4.2 %all-to-all-start = ((bf16[32,2,512]{2,0,1:T(8,128)(2,1)}), bf16[32,2,512]{2,0,1:T(8,128)(2,1)S(1)}, u32[]{:S(2)}, u32[]{:S(2)}) async-start(bf16[32,2,512]{2,0,1:T(8,128)(2,1)} %bitcast.31), calls=%async_computation | async-start | bytes 131072 | tf_op jit(solution)/shard_map/all_to_all | solution.py:33
  6.5 0.8 %select_reduce_fusion = s32[64,4]{0,1:T(4,128)S(1)} fusion(s32[4,4]{1,0:T(4,128)} %param.14, pred[64,4]{0,1:T(4,128)(4,1)S(1)} %iota_compare_fusion.3), kind=kLoop, calls=%fused_computation.33 | loop fusion | flops 1792 | bytes 1344 | tf_op jit(solution)/shard_map/reduce_sum | solution.py:44
  7.3 0.7 %select_reduce_fusion.1 = s32[256]{0:T(256)S(1)} fusion(s32[4]{0:T(128)} %param.15, s32[256]{0:T(256)S(1)} %and_select_fusion.2), kind=kLoop, calls=%fused_computation.34 | loop fusion | flops 2816 | bytes 2064 | tf_op jit(solution)/shard_map/while/body/eval_jaxpr/reduce_sum | solution.py:51
  8.1 0.1 iota_compare_fusion.2
  8.2 0.8 %select_reduce_fusion.2 = (s32[64]{0:T(128)S(1)}, s32[64]{0:T(128)S(1)}) fusion(s32[4]{0:T(128)} %param.13, s32[64]{0:T(128)S(1)} %and_select_fusion.3, s32[4]{0:T(128)} %param.15), kind=kLoop, calls=%fused_computation.37 | loop fusion | flops 1152 | bytes 800 | tf_op jit(solution)/shard_map/reduce_sum | solution.py:45
  9.0 0.6 %and_reduce_fusion.2 = pred[]{:T(512)} fusion(pred[4]{0:T(512)(128)(4,1)S(1)} %get-tuple-element.148, pred[4]{0:T(512)(128)(4,1)S(1)} %get-tuple-element.158), kind=kLoop, calls=%fused_computation.43 | loop fusion | flops 7 | bytes 9 | tf_op jit(solution)/shard_map/while/body/eval_jaxpr/reduce_or | solution.py:60
  9.6 1.5 %copy.70 = bf16[4,2,8,512]{3,2,0,1:T(8,128)(2,1)} copy(bf16[4,2,8,512]{3,2,1,0:T(8,128)(2,1)} %bitcast.41) | data formatting | bytes 131072 | tf_op jit(solution)/shard_map/all_to_all | solution.py:34
  11.1 3.3 %all-to-all-start.2 = ((bf16[32,2,512]{2,0,1:T(8,128)(2,1)}), bf16[32,2,512]{2,0,1:T(8,128)(2,1)S(1)}, u32[]{:S(2)}, u32[]{:S(2)}) async-start(bf16[32,2,512]{2,0,1:T(8,128)(2,1)} %bitcast.30), calls=%async_computation.2 | async-start | bytes 131072 | tf_op jit(solution)/shard_map/all_to_all | solution.py:34
  15.1 1.8 %copy.69 = bf16[4,2,8,3072]{3,2,0,1:T(8,128)(2,1)} copy(bf16[4,2,8,3072]{3,2,1,0:T(8,128)(2,1)} %bitcast.35) | data formatting | bytes 786432 | tf_op jit(solution)/shard_map/all_to_all | solution.py:32
  16.9 1.6 %all-to-all-done.2 = bf16[32,2,512]{2,0,1:T(8,128)(2,1)S(1)} async-done(((bf16[32,2,512]{2,0,1:T(8,128)(2,1)}), bf16[32,2,512]{2,0,1:T(8,128)(2,1)S(1)}, u32[]{:S(2)}, u32[]{:S(2)}) %all-to-all-start.2) | async-done | bytes 65568 | tf_op jit(solution)/shard_map/all_to_all | solution.py:34
  18.5 3.5 %all-to-all-start.1 = ((bf16[32,2,3072]{2,0,1:T(8,128)(2,1)}), bf16[32,2,3072]{2,0,1:T(8,128)(2,1)S(1)}, u32[]{:S(2)}, u32[]{:S(2)}) async-start(bf16[32,2,3072]{2,0,1:T(8,128)(2,1)} %bitcast.29), calls=%async_computation.1 | async-start | bytes 786432 | tf_op jit(solution)/shard_map/all_to_all | solution.py:32
  22.0 6.3 %all_gather.6 = bf16[256,512]{1,0:T(8,128)(2,1)S(1)} all-gather(bf16[64,512]{1,0:T(8,128)(2,1)S(1)} %bitcast.37), channel_id=1, replica_groups=mesh['ctx'=4,'head'=2,'dp'=4] {'ctx'}, dimensions={0}, use_global_device_ids=true | all-gather | bytes 327680 | tf_op jit(solution)/shard_map/all_gather | solution.py:109
  28.3 5.8 %all_gather.7 = bf16[256,512]{1,0:T(8,128)(2,1)S(1)} all-gather(bf16[64,512]{1,0:T(8,128)(2,1)S(1)} %bitcast.38), channel_id=1, replica_groups=mesh['ctx'=4,'head'=2,'dp'=4] {'ctx'}, dimensions={0}, use_global_device_ids=true | all-gather | bytes 327680 | tf_op jit(solution)/shard_map/all_gather | solution.py:110
  34.2 6.7 %conditional.1 = ((f32[64,4,6]{0,2,1:T(8,128)S(1)}, f32[64,4,6,128]{3,0,2,1:T(8,128)S(1)})) conditional(s32[]{:T(128)} %convert_element_type.13, (f32[64,4,6]{0,2,1:T(8,128)S(1)}, f32[64,4,6,128]{3,0,2,1:T(8,128)S(1)}) %tuple.31, (pred[64,4]{0,1:T(4,128)(4,1)S(1)}, pred[256,4]{0,1:T(4,128)(4,1)S(1)}, s32[256]{0:T(256)S(1)}, s32[256]{0:T(256)S(1)}, ...), branch_computations={%region_6.7_spmd, %region_7.11_spmd} | conditional | flops 205395968 | bytes 9220888 | solution.py:94
  34.2 1.3 %reshape.148 = bf16[64,4,6,128]{3,2,1,0:T(8,128)(2,1)} reshape(bf16[2,32,3072]{2,1,0:T(8,128)(2,1)S(1)} %get-tuple-element.127) | data formatting | bytes 786432 | tf_op jit(solution)/shard_map/reshape | solution.py:39
  35.4 0.8 %reshape.147 = bf16[256,4,128]{2,1,0:T(4,128)(2,1)} reshape(bf16[256,512]{1,0:T(8,128)(2,1)S(1)} %get-tuple-element.126) | data formatting | bytes 524288 | tf_op jit(solution)/shard_map/while/body/eval_jaxpr/reshape | solution.py:54
  36.4 1.6 %fusion.21 = (f32[64,4,6]{0,2,1:T(8,128)S(1)}, f32[64,4,6,256]{3,0,2,1:T(8,128)S(1)}) fusion(bf16[64,4,6,128]{3,2,1,0:T(8,128)(2,1)} %reshape.148, bf16[256,4,128,1]{2,1,0,3:T(4,128)(2,1)} %bitcast.39, pred[64,256]{1,0:T(8,128)(4,1)S(1)} %broadcast_and_fusion), kind=kOutput, calls=%fused_computation.57 | convolution fusion | flops 101841408 | bytes 2250752 | tf_op jit(solution)/shard_map/while/body/eval_jaxpr/cond/branch_1_fun/rkgd,nkd->rkgn/dot_general | solution.py:69
  38.0 0.5 fusion.2
  38.6 0.8 %reshape.149 = bf16[256,4,128]{2,1,0:T(4,128)(2,1)} reshape(bf16[256,512]{1,0:T(8,128)(2,1)S(1)} %get-tuple-element.129) | data formatting | bytes 524288 | tf_op jit(solution)/shard_map/while/body/eval_jaxpr/reshape | solution.py:55
  39.3 1.6 %fusion = f32[64,4,6,128]{3,0,2,1:T(8,128)S(1)} fusion(f32[64,4,6,256]{3,0,2,1:T(8,128)S(1)} %get-tuple-element.153, f32[64,4,6,128]{3,0,2,1:T(8,128)S(1)} %get-tuple-element.128, f32[64,4,6]{0,2,1:T(8,128)S(1)} %broadcast_maximum_fusion, pred[64,256]{1,0:T(8,128)(4,1)S(1)} %broadcast_and_fusion, f32[64,4,6]{0,2,1:T(8,128)S(1)} %get-tuple-element.150, ...), kind=kOutput, calls=%fused_computation.3 | convolution fusion | flops 102236160 | bytes 3436544 | tf_op jit(solution)/shard_map/while/body/eval_jaxpr/cond/branch_1_fun/rkgn,nkd->rkgd/dot_general | solution.py:83
  40.9 0.3 broadcast_divide_fusion
  41.2 0.5 copy.44
  41.7 0.2 reshape.151
  41.9 1.3 %broadcast_select_fusion = (bf16[64,3072]{1,0:T(8,128)(2,1)S(1)}, bf16[64,3072]{1,0:T(8,128)(2,1)}) fusion(pred[]{:T(512)S(6)} %lt.53, f32[64,3072]{1,0:T(8,128)S(1)} %reshape.151, f32[64,3072]{1,0:T(8,128)S(1)} %copy-done, s32[64]{0:T(128)S(1)} %get-tuple-element.146, pred[64]{0:T(512)(128)(4,1)S(1)} %fusion.19), kind=kOutput, calls=%fused_computation.25 | convolution fusion | flops 151785472 | bytes 2359617 | tf_op jit(solution)/shard_map/dot_general | solution.py:124
  43.2 3.4 %collective-permute-start = (bf16[16,3072]{1,0:T(8,128)(2,1)S(1)}, bf16[16,3072]{1,0:T(8,128)(2,1)S(1)}, u32[]{:S(2)}, u32[]{:S(2)}) collective-permute-start(bf16[16,3072]{1,0:T(8,128)(2,1)S(1)} %get-tuple-element.156), channel_id=1, source_target_pairs={{0,24},{1,25},{2,26},{3,27},{4,28},{5,29},{6,30},{7,31}} | collective-permute-start | bytes 294920 | tf_op jit(solution)/shard_map/ppermute | solution.py:17
  46.6 1.3 %collective-permute-start.1 = (bf16[16,3072]{1,0:T(8,128)(2,1)S(1)}, bf16[16,3072]{1,0:T(8,128)(2,1)S(1)}, u32[]{:S(2)}, u32[]{:S(2)}) collective-permute-start(bf16[16,3072]{1,0:T(8,128)(2,1)S(1)} %get-tuple-element.155), channel_id=1, source_target_pairs={{0,16},{8,24},{1,17},{9,25},{2,18},{10,26},{3,19},{11,27},{4,20},{... | collective-permute-start | bytes 294920 | tf_op jit(solution)/shard_map/ppermute | solution.py:17
  47.9 2.0 %collective-permute-start.2 = (bf16[16,3072]{1,0:T(8,128)(2,1)S(1)}, bf16[16,3072]{1,0:T(8,128)(2,1)S(1)}, u32[]{:S(2)}, u32[]{:S(2)}) collective-permute-start(bf16[16,3072]{1,0:T(8,128)(2,1)S(1)} %get-tuple-element.154), channel_id=1, source_target_pairs={{0,8},{8,16},{16,24},{1,9},{9,17},{17,25},{2,10},{10,18},{18,26},{... | collective-permute-start | bytes 294920 | tf_op jit(solution)/shard_map/ppermute | solution.py:17
  50.0 3.5 %all-to-all-start.3 = ((bf16[2,32,3072]{2,1,0:T(8,128)(2,1)}), bf16[2,32,3072]{2,1,0:T(8,128)(2,1)S(1)}, u32[]{:S(2)}, u32[]{:S(2)}) async-start(bf16[2,32,3072]{2,1,0:T(8,128)(2,1)} %bitcast.9), calls=%async_computation.3 | async-start | bytes 786432 | tf_op jit(solution)/shard_map/all_to_all | solution.py:131
  53.5 0.7 %fusion.15 = bf16[16,3072]{1,0:T(8,128)(2,1)} fusion(bf16[16,3072]{1,0:T(8,128)(2,1)S(1)} %collective-permute-done, bf16[16,3072]{1,0:T(8,128)(2,1)S(1)} %collective-permute-done.1, bf16[16,3072]{1,0:T(8,128)(2,1)S(1)} %collective-permute-done.2, bf16[64,3072]{1,0:T(8,128)(2,1)S(1)} %get-tuple-element.159, pred[]{:T(512)S(6)} %eq.97, pred[]{:T(512)S(6)} %eq.96, ...), kind=kLoop, calls=%fused_computation.28 | loop fusion | flops 147456 | bytes 491523 | tf_op jit(solution)/shard_map/jit(_where)/select_n | solution.py:151
  54.1 6.6 %all-to-all-done.3 = bf16[2,32,3072]{2,1,0:T(8,128)(2,1)S(1)} async-done(((bf16[2,32,3072]{2,1,0:T(8,128)(2,1)}), bf16[2,32,3072]{2,1,0:T(8,128)(2,1)S(1)}, u32[]{:S(2)}, u32[]{:S(2)}) %all-to-all-start.3) | async-done | bytes 393248 | tf_op jit(solution)/shard_map/all_to_all | solution.py:131
  60.7 0.8 %copy.55 = bf16[2,4,8,3072]{3,2,0,1:T(8,128)(2,1)} copy(bf16[2,4,8,3072]{3,2,1,0:T(8,128)(2,1)S(1)} %bitcast.33) | data formatting | bytes 786432 | tf_op jit(solution)/shard_map/all_to_all | solution.py:131
  (23 shorter events, 0.4 us)
Async XLA Ops:
  0.6 41.2 %copy-start = (f32[64,3072]{1,0:T(8,128)S(1)}, f32[64,3072]{1,0:T(8,128)}, u32[]{:S(2)}) copy-start(f32[64,3072]{1,0:T(8,128)} %param.12) | copy-start | bytes 2359300
  2.2 8.9 %all-to-all-start = ((bf16[32,2,512]{2,0,1:T(8,128)(2,1)}), bf16[32,2,512]{2,0,1:T(8,128)(2,1)S(1)}, u32[]{:S(2)}, u32[]{:S(2)}) async-start(bf16[32,2,512]{2,0,1:T(8,128)(2,1)} %bitcast.31), calls=%async_computation | async-start | bytes 131072 | tf_op jit(solution)/shard_map/all_to_all | solution.py:33
  11.1 7.4 %all-to-all-start.2 = ((bf16[32,2,512]{2,0,1:T(8,128)(2,1)}), bf16[32,2,512]{2,0,1:T(8,128)(2,1)S(1)}, u32[]{:S(2)}, u32[]{:S(2)}) async-start(bf16[32,2,512]{2,0,1:T(8,128)(2,1)} %bitcast.30), calls=%async_computation.2 | async-start | bytes 131072 | tf_op jit(solution)/shard_map/all_to_all | solution.py:34
  18.5 15.6 %all-to-all-start.1 = ((bf16[32,2,3072]{2,0,1:T(8,128)(2,1)}), bf16[32,2,3072]{2,0,1:T(8,128)(2,1)S(1)}, u32[]{:S(2)}, u32[]{:S(2)}) async-start(bf16[32,2,3072]{2,0,1:T(8,128)(2,1)} %bitcast.29), calls=%async_computation.1 | async-start | bytes 786432 | tf_op jit(solution)/shard_map/all_to_all | solution.py:32
  43.2 10.2 %collective-permute-start = (bf16[16,3072]{1,0:T(8,128)(2,1)S(1)}, bf16[16,3072]{1,0:T(8,128)(2,1)S(1)}, u32[]{:S(2)}, u32[]{:S(2)}) collective-permute-start(bf16[16,3072]{1,0:T(8,128)(2,1)S(1)} %get-tuple-element.156), channel_id=1, source_target_pairs={{0,24},{1,25},{2,26},{3,27},{4,28},{5,29},{6,30},{7,31}} | collective-permute-start | bytes 294920 | tf_op jit(solution)/shard_map/ppermute | solution.py:17
  46.6 6.8 %collective-permute-start.1 = (bf16[16,3072]{1,0:T(8,128)(2,1)S(1)}, bf16[16,3072]{1,0:T(8,128)(2,1)S(1)}, u32[]{:S(2)}, u32[]{:S(2)}) collective-permute-start(bf16[16,3072]{1,0:T(8,128)(2,1)S(1)} %get-tuple-element.155), channel_id=1, source_target_pairs={{0,16},{8,24},{1,17},{9,25},{2,18},{10,26},{3,19},{11,27},{4,20},{... | collective-permute-start | bytes 294920 | tf_op jit(solution)/shard_map/ppermute | solution.py:17
  47.9 5.6 %collective-permute-start.2 = (bf16[16,3072]{1,0:T(8,128)(2,1)S(1)}, bf16[16,3072]{1,0:T(8,128)(2,1)S(1)}, u32[]{:S(2)}, u32[]{:S(2)}) collective-permute-start(bf16[16,3072]{1,0:T(8,128)(2,1)S(1)} %get-tuple-element.154), channel_id=1, source_target_pairs={{0,8},{8,16},{16,24},{1,9},{9,17},{17,25},{2,10},{10,18},{18,26},{... | collective-permute-start | bytes 294920 | tf_op jit(solution)/shard_map/ppermute | solution.py:17
  50.0 10.7 %all-to-all-start.3 = ((bf16[2,32,3072]{2,1,0:T(8,128)(2,1)}), bf16[2,32,3072]{2,1,0:T(8,128)(2,1)S(1)}, u32[]{:S(2)}, u32[]{:S(2)}) async-start(bf16[2,32,3072]{2,1,0:T(8,128)(2,1)} %bitcast.9), calls=%async_computation.3 | async-start | bytes 786432 | tf_op jit(solution)/shard_map/all_to_all | solution.py:131
where the time goes:
time: 62.2 us; the launch traced here: 61.5 us
  starting transfers between devices  21.2 us (34%)
  blocking collectives  12.1 us (19%)
  local copies, waits for them, and re-layouts  9.12 us (15%)
  waiting for transfers between devices  8.19 us (13%)
  other arithmetic  4.82 us (8%)
  matrix products  4.5 us (7%)
  between operations  1.43 us (2%)
    ppermute x3, starting transfers between devices, from_behind(): return lax.ppermute(block, axis, route)  6.7 us
    all_to_all x1, waiting for transfers between devices, body(): lax.all_to_all(gated, 'head', split_axis=0, concat_axis=1, tiled=True)  6.56 us
    all_gather x1, blocking collectives, body(): key_piece = lax.all_gather(key_local, 'ctx', axis=0, tiled=True)  6.31 us
    all_gather x1, blocking collectives, body(): value_piece = lax.all_gather(value_local, 'ctx', axis=0, tiled=True)  5.84 us
    all_to_all x1, starting transfers between devices, body(): lax.all_to_all(keys, 'head', split_axis=1, concat_axis=0, tiled=True)  4.23 us
    all_to_all x1, starting transfers between devices, body(): lax.all_to_all(gated, 'head', split_axis=0, concat_axis=1, tiled=True)  3.48 us
    all_to_all x1, starting transfers between devices, body(): lax.all_to_all(queries, 'head', split_axis=1, concat_axis=0, tiled=True)  3.47 us
    all_to_all x1, starting transfers between devices, body(): lax.all_to_all(values, 'head', split_axis=1, concat_axis=0, tiled=True)  3.32 us
  transfers between devices with their start and end apart: 7, of which 2 were waited for; matrix products, arithmetic and copies ran while one was open for 12% of the time, Pallas kernels for 0%

commit v1 on v0

--- a/solution.py
+++ b/solution.py
@@ -106,8 +106,15 @@
         jnp.zeros((rows_ctx, local_kv_heads, heads_per_group), jnp.float32),
         jnp.zeros((rows_ctx, local_kv_heads, heads_per_group, HEAD_SIZE), jnp.float32),
     )
-    key_piece = lax.all_gather(key_local, "ctx", axis=0, tiled=True)
-    value_piece = lax.all_gather(value_local, "ctx", axis=0, tiled=True)
+
+    def spots_move(local, point):
+        return jnp.split(
+            lax.all_gather(jnp.concatenate([local, point], axis=1), "ctx", axis=0, tiled=True),
+            [local.shape[1]],
+            1,
+        )
+
+    key_piece, value_piece = spots_move(key_local, value_local)
     piece_rows = key_piece.shape[0]
     block_rows = math.gcd(piece_rows, 512)
 

time: 62.2 us -> 53 us (0.85)
  blocking collectives: 12.1 us -> 7.73 us
  local copies, waits for them, and re-layouts: 9.12 us -> 7.04 us
  matrix products: 4.5 us -> 2.46 us
  starting transfers between devices: 21.2 us -> 20.5 us
    all_gather x2 -> x1, blocking collectives: 12.1 us -> 7.73 us  [spots_move(): lax.all_gather(jnp.concatenate([local, point], axis=1), 'ctx', axis=0, ti...]
    all_to_all x1, waiting for transfers between devices: 0.01 us -> 1.61 us  [body(): lax.all_to_all(keys, 'head', split_axis=1, concat_axis=0, tiled=True)]
    all_to_all x1, waiting for transfers between devices: 1.61 us -> 0.01 us  [body(): lax.all_to_all(values, 'head', split_axis=1, concat_axis=0, tiled=True)]
    reshape x2 -> x0, local copies, waits for them, and re-layouts: 1.53 us -> none  [the longest x1 0.77 us: key_block(): value_head_rows = value_block_rows.reshape(block_rows, -1, HEAD_SIZE)]
    dot_general x1, matrix products: 1.63 us -> 0.48 us  [update(): jnp.einsum('rkgd,nkd->rkgn', query_grouped, key_head_rows, preferred_elem...]
    all_to_all x1, starting transfers between devices: 4.23 us -> 3.32 us  [body(): lax.all_to_all(keys, 'head', split_axis=1, concat_axis=0, tiled=True)]
    all_to_all x1, starting transfers between devices: 3.32 us -> 4.23 us  [body(): lax.all_to_all(values, 'head', split_axis=1, concat_axis=0, tiled=True)]
    dot_general x1, matrix products: 1.56 us -> 0.67 us  [update(): jnp.einsum('rkgn,nkd->rkgd', weights.astype(jnp.bfloat16), value_head_row...]
  transfers between devices with their start and end apart: 7 -> 7, of which waited for: 2 -> 2; matrix products, arithmetic and copies ran while one was open for 12% -> 14% of each run, Pallas kernels for 0% -> 0%
where the time goes in v1:
time: 53 us; the launch traced here: 52.3 us
  starting transfers between devices  20.5 us (39%)
  waiting for transfers between devices  8.22 us (16%)
  blocking collectives  7.73 us (15%)
  local copies, waits for them, and re-layouts  7.04 us (13%)
  other arithmetic  4.85 us (9%)
  matrix products  2.46 us (5%)
  between operations  1.44 us (3%)
    all_gather x1, blocking collectives, spots_move(): lax.all_gather(jnp.concatenate([local, point], axis=1), 'ctx', axis=0, ti...  7.73 us
    all_to_all x1, waiting for transfers between devices, body(): lax.all_to_all(gated, 'head', split_axis=0, concat_axis=1, tiled=True)  6.59 us
    ppermute x3, starting transfers between devices, from_behind(): return lax.ppermute(block, axis, route)  6 us
    all_to_all x1, starting transfers between devices, body(): lax.all_to_all(values, 'head', split_axis=1, concat_axis=0, tiled=True)  4.23 us
    all_to_all x1, starting transfers between devices, body(): lax.all_to_all(gated, 'head', split_axis=0, concat_axis=1, tiled=True)  3.48 us
    all_to_all x1, starting transfers between devices, body(): lax.all_to_all(queries, 'head', split_axis=1, concat_axis=0, tiled=True)  3.47 us
    all_to_all x1, starting transfers between devices, body(): lax.all_to_all(keys, 'head', split_axis=1, concat_axis=0, tiled=True)  3.32 us
    all_to_all x1, local copies, waits for them, and re-layouts, body(): lax.all_to_all(queries, 'head', split_axis=1, concat_axis=0, tiled=True)  1.77 us
  transfers between devices with their start and end apart: 7, of which 2 were waited for; matrix products, arithmetic and copies ran while one was open for 14% of the time, Pallas kernels for 0%

profile of v1, /device:TPU:0, one launch (start us, length us, event | category | flops | bytes accessed | tf_op | source)
XLA Modules:
  0.0 52.3 jit_solution(1430453020769166919)
XLA Ops:
  0.6 1.5 %copy.84 = bf16[4,2,8,512]{3,2,0,1:T(8,128)(2,1)} copy(bf16[4,2,8,512]{3,2,1,0:T(8,128)(2,1)} %bitcast.50) | data formatting | bytes 131072 | tf_op jit(solution)/shard_map/all_to_all | solution.py:34
  2.2 4.2 %all-to-all-start.1 = ((bf16[32,2,512]{2,0,1:T(8,128)(2,1)}), bf16[32,2,512]{2,0,1:T(8,128)(2,1)S(1)}, u32[]{:S(2)}, u32[]{:S(2)}) async-start(bf16[32,2,512]{2,0,1:T(8,128)(2,1)} %bitcast.40), calls=%async_computation.1 | async-start | bytes 131072 | tf_op jit(solution)/shard_map/all_to_all | solution.py:34
  6.5 0.8 %select_reduce_fusion = s32[64,4]{0,1:T(4,128)S(1)} fusion(s32[4,4]{1,0:T(4,128)} %param.14, pred[64,4]{0,1:T(4,128)(4,1)S(1)} %iota_compare_fusion.3), kind=kLoop, calls=%fused_computation.32 | loop fusion | flops 1792 | bytes 1344 | tf_op jit(solution)/shard_map/reduce_sum | solution.py:44
  7.2 0.1 fusion.18
  7.3 0.7 %select_reduce_fusion.1 = s32[256]{0:T(256)S(1)} fusion(s32[4]{0:T(128)} %param.15, s32[256]{0:T(256)S(1)} %and_select_fusion.2), kind=kLoop, calls=%fused_computation.33 | loop fusion | flops 2816 | bytes 2064 | tf_op jit(solution)/shard_map/while/body/eval_jaxpr/reduce_sum | solution.py:51
  8.1 0.1 iota_compare_fusion.2
  8.2 0.8 %select_reduce_fusion.2 = (s32[64]{0:T(128)S(1)}, s32[64]{0:T(128)S(1)}) fusion(s32[4]{0:T(128)} %param.13, s32[64]{0:T(128)S(1)} %and_select_fusion.3, s32[4]{0:T(128)} %param.15), kind=kLoop, calls=%fused_computation.36 | loop fusion | flops 1152 | bytes 800 | tf_op jit(solution)/shard_map/reduce_sum | solution.py:45
  9.0 0.6 %and_reduce_fusion.2 = pred[]{:T(512)} fusion(pred[4]{0:T(512)(128)(4,1)S(1)} %get-tuple-element.183, pred[4]{0:T(512)(128)(4,1)S(1)} %get-tuple-element.195), kind=kLoop, calls=%fused_computation.42 | loop fusion | flops 7 | bytes 9 | tf_op jit(solution)/shard_map/while/body/eval_jaxpr/reduce_or | solution.py:60
  9.6 1.5 %copy.85 = bf16[4,2,8,512]{3,2,0,1:T(8,128)(2,1)} copy(bf16[4,2,8,512]{3,2,1,0:T(8,128)(2,1)} %bitcast.51) | data formatting | bytes 131072 | tf_op jit(solution)/shard_map/all_to_all | solution.py:33
  11.1 3.3 %all-to-all-start = ((bf16[32,2,512]{2,0,1:T(8,128)(2,1)}), bf16[32,2,512]{2,0,1:T(8,128)(2,1)S(1)}, u32[]{:S(2)}, u32[]{:S(2)}) async-start(bf16[32,2,512]{2,0,1:T(8,128)(2,1)} %bitcast.41), calls=%async_computation | async-start | bytes 131072 | tf_op jit(solution)/shard_map/all_to_all | solution.py:33
  15.1 1.8 %copy.83 = bf16[4,2,8,3072]{3,2,0,1:T(8,128)(2,1)} copy(bf16[4,2,8,3072]{3,2,1,0:T(8,128)(2,1)} %bitcast.46) | data formatting | bytes 786432 | tf_op jit(solution)/shard_map/all_to_all | solution.py:32
  16.9 1.6 %all-to-all-done = bf16[32,2,512]{2,0,1:T(8,128)(2,1)S(1)} async-done(((bf16[32,2,512]{2,0,1:T(8,128)(2,1)}), bf16[32,2,512]{2,0,1:T(8,128)(2,1)S(1)}, u32[]{:S(2)}, u32[]{:S(2)}) %all-to-all-start) | async-done | bytes 65568 | tf_op jit(solution)/shard_map/all_to_all | solution.py:33
  18.5 3.5 %all-to-all-start.2 = ((bf16[32,2,3072]{2,0,1:T(8,128)(2,1)}), bf16[32,2,3072]{2,0,1:T(8,128)(2,1)S(1)}, u32[]{:S(2)}, u32[]{:S(2)}) async-start(bf16[32,2,3072]{2,0,1:T(8,128)(2,1)} %bitcast.39), calls=%async_computation.2 | async-start | bytes 786432 | tf_op jit(solution)/shard_map/all_to_all | solution.py:32
  22.0 7.7 %all_gather.3 = bf16[256,1024]{1,0:T(8,128)(2,1)S(1)} all-gather(bf16[64,1024]{1,0:T(8,128)(2,1)S(1)} %pad_maximum_fusion), channel_id=1, replica_groups=mesh['ctx'=4,'head'=2,'dp'=4] {'ctx'}, dimensions={0}, use_global_device_ids=true | all-gather | bytes 655360 | tf_op jit(solution)/shard_map/all_gather | solution.py:112
  29.8 2.6 %conditional.1 = ((f32[64,4,6]{0,2,1:T(8,128)S(1)}, f32[64,4,6,128]{3,0,2,1:T(8,128)S(1)})) conditional(s32[]{:T(128)} %convert_element_type.13, (f32[64,4,6]{0,2,1:T(8,128)S(1)}, f32[64,4,6,128]{3,0,2,1:T(8,128)S(1)}) %tuple.32, (pred[64,4]{0,1:T(4,128)(4,1)S(1)}, pred[256,4]{0,1:T(4,128)(4,1)S(1)}, s32[256]{0:T(256)S(1)}, s32[256]{0:T(256)S(1)}, ...), branch_computations={%region_6.7_spmd, %region_7.11_spmd} | conditional | flops 205395968 | bytes 10269464 | solution.py:94
  29.8 0.2 copy.63
  30.0 0.5 reshape.148
  30.5 0.1 and_reduce_fusion
  30.7 0.5 fusion.20
  31.2 0.6 %fusion.2 = f32[64,4,6]{0,2,1:T(8,128)S(1)} fusion(f32[64,4,6,256]{3,0,2,1:T(8,128)S(1)} %get-tuple-element.190, f32[64,4,6]{0,2,1:T(8,128)S(1)} %broadcast_maximum_fusion, pred[64,256]{1,0:T(8,128)(4,1)S(1)} %broadcast_and_fusion), kind=kLoop, calls=%fused_computation.5 | loop fusion | flops 1178112 | bytes 1601536 | tf_op jit(solution)/shard_map/while/body/eval_jaxpr/cond/branch_1_fun/reduce_sum | solution.py:82
  31.7 0.7 %fusion = f32[64,4,6,128]{3,0,2,1:T(8,128)S(1)} fusion(bf16[256,4,128,1]{0,2,3,1:T(8,128)(2,1)S(1)} %bitcast.45, f32[64,4,6,256]{3,0,2,1:T(8,128)S(1)} %get-tuple-element.190, f32[64,4,6,128]{3,0,2,1:T(8,128)S(1)} %get-tuple-element.129, f32[64,4,6]{0,2,1:T(8,128)S(1)} %broadcast_maximum_fusion, pred[64,256]{1,0:T(8,128)(4,1)S(1)} %broadcast_and_fusion, ...), kind=kOutput, calls=%fused_computation.3 | convolution fusion | flops 102236160 | bytes 3436544 | tf_op jit(solution)/shard_map/while/body/eval_jaxpr/cond/branch_1_fun/rkgn,nkd->rkgd/dot_general | solution.py:83
  32.4 0.3 broadcast_divide_fusion
  32.7 0.5 copy.64
  33.2 0.2 reshape.151
  33.4 1.3 %broadcast_select_fusion = (bf16[64,3072]{1,0:T(8,128)(2,1)S(1)}, bf16[64,3072]{1,0:T(8,128)(2,1)}) fusion(pred[]{:T(512)S(6)} %lt.53, f32[64,3072]{1,0:T(8,128)S(1)} %reshape.151, f32[64,3072]{1,0:T(8,128)S(1)} %copy-done, s32[64]{0:T(128)S(1)} %get-tuple-element.181, pred[64]{0:T(512)(128)(4,1)S(1)} %fusion.17), kind=kOutput, calls=%fused_computation.23 | convolution fusion | flops 151785472 | bytes 2359617 | tf_op jit(solution)/shard_map/dot_general | solution.py:131
  34.7 2.7 %collective-permute-start = (bf16[16,3072]{1,0:T(8,128)(2,1)S(1)}, bf16[16,3072]{1,0:T(8,128)(2,1)S(1)}, u32[]{:S(2)}, u32[]{:S(2)}) collective-permute-start(bf16[16,3072]{1,0:T(8,128)(2,1)S(1)} %get-tuple-element.193), channel_id=1, source_target_pairs={{0,24},{1,25},{2,26},{3,27},{4,28},{5,29},{6,30},{7,31}} | collective-permute-start | bytes 294920 | tf_op jit(solution)/shard_map/ppermute | solution.py:17
  37.4 1.3 %collective-permute-start.1 = (bf16[16,3072]{1,0:T(8,128)(2,1)S(1)}, bf16[16,3072]{1,0:T(8,128)(2,1)S(1)}, u32[]{:S(2)}, u32[]{:S(2)}) collective-permute-start(bf16[16,3072]{1,0:T(8,128)(2,1)S(1)} %get-tuple-element.192), channel_id=1, source_target_pairs={{0,16},{8,24},{1,17},{9,25},{2,18},{10,26},{3,19},{11,27},{4,20},{... | collective-permute-start | bytes 294920 | tf_op jit(solution)/shard_map/ppermute | solution.py:17
  38.7 2.0 %collective-permute-start.2 = (bf16[16,3072]{1,0:T(8,128)(2,1)S(1)}, bf16[16,3072]{1,0:T(8,128)(2,1)S(1)}, u32[]{:S(2)}, u32[]{:S(2)}) collective-permute-start(bf16[16,3072]{1,0:T(8,128)(2,1)S(1)} %get-tuple-element.191), channel_id=1, source_target_pairs={{0,8},{8,16},{16,24},{1,9},{9,17},{17,25},{2,10},{10,18},{18,26},{... | collective-permute-start | bytes 294920 | tf_op jit(solution)/shard_map/ppermute | solution.py:17
  40.8 3.5 %all-to-all-start.3 = ((bf16[2,32,3072]{2,1,0:T(8,128)(2,1)}), bf16[2,32,3072]{2,1,0:T(8,128)(2,1)S(1)}, u32[]{:S(2)}, u32[]{:S(2)}) async-start(bf16[2,32,3072]{2,1,0:T(8,128)(2,1)} %bitcast.11), calls=%async_computation.3 | async-start | bytes 786432 | tf_op jit(solution)/shard_map/all_to_all | solution.py:138
  44.3 0.7 %fusion.13 = bf16[16,3072]{1,0:T(8,128)(2,1)} fusion(bf16[16,3072]{1,0:T(8,128)(2,1)S(1)} %collective-permute-done, bf16[16,3072]{1,0:T(8,128)(2,1)S(1)} %collective-permute-done.1, bf16[16,3072]{1,0:T(8,128)(2,1)S(1)} %collective-permute-done.2, bf16[64,3072]{1,0:T(8,128)(2,1)S(1)} %get-tuple-element.196, pred[]{:T(512)S(6)} %eq.97, pred[]{:T(512)S(6)} %eq.96, ...), kind=kLoop, calls=%fused_computation.27 | loop fusion | flops 147456 | bytes 491523 | tf_op jit(solution)/shard_map/jit(_where)/select_n | solution.py:158
  44.9 6.6 %all-to-all-done.3 = bf16[2,32,3072]{2,1,0:T(8,128)(2,1)S(1)} async-done(((bf16[2,32,3072]{2,1,0:T(8,128)(2,1)}), bf16[2,32,3072]{2,1,0:T(8,128)(2,1)S(1)}, u32[]{:S(2)}, u32[]{:S(2)}) %all-to-all-start.3) | async-done | bytes 393248 | tf_op jit(solution)/shard_map/all_to_all | solution.py:138
  51.5 0.8 %copy.75 = bf16[2,4,8,3072]{3,2,0,1:T(8,128)(2,1)} copy(bf16[2,4,8,3072]{3,2,1,0:T(8,128)(2,1)S(1)} %bitcast.43) | data formatting | bytes 786432 | tf_op jit(solution)/shard_map/all_to_all | solution.py:138
  (23 shorter events, 0.3 us)
Async XLA Ops:
  0.6 32.8 %copy-start = (f32[64,3072]{1,0:T(8,128)S(1)}, f32[64,3072]{1,0:T(8,128)}, u32[]{:S(2)}) copy-start(f32[64,3072]{1,0:T(8,128)} %param.12) | copy-start | bytes 2359300
  2.2 8.9 %all-to-all-start.1 = ((bf16[32,2,512]{2,0,1:T(8,128)(2,1)}), bf16[32,2,512]{2,0,1:T(8,128)(2,1)S(1)}, u32[]{:S(2)}, u32[]{:S(2)}) async-start(bf16[32,2,512]{2,0,1:T(8,128)(2,1)} %bitcast.40), calls=%async_computation.1 | async-start | bytes 131072 | tf_op jit(solution)/shard_map/all_to_all | solution.py:34
  11.1 7.4 %all-to-all-start = ((bf16[32,2,512]{2,0,1:T(8,128)(2,1)}), bf16[32,2,512]{2,0,1:T(8,128)(2,1)S(1)}, u32[]{:S(2)}, u32[]{:S(2)}) async-start(bf16[32,2,512]{2,0,1:T(8,128)(2,1)} %bitcast.41), calls=%async_computation | async-start | bytes 131072 | tf_op jit(solution)/shard_map/all_to_all | solution.py:33
  18.5 11.2 %all-to-all-start.2 = ((bf16[32,2,3072]{2,0,1:T(8,128)(2,1)}), bf16[32,2,3072]{2,0,1:T(8,128)(2,1)S(1)}, u32[]{:S(2)}, u32[]{:S(2)}) async-start(bf16[32,2,3072]{2,0,1:T(8,128)(2,1)} %bitcast.39), calls=%async_computation.2 | async-start | bytes 786432 | tf_op jit(solution)/shard_map/all_to_all | solution.py:32
  34.7 9.5 %collective-permute-start = (bf16[16,3072]{1,0:T(8,128)(2,1)S(1)}, bf16[16,3072]{1,0:T(8,128)(2,1)S(1)}, u32[]{:S(2)}, u32[]{:S(2)}) collective-permute-start(bf16[16,3072]{1,0:T(8,128)(2,1)S(1)} %get-tuple-element.193), channel_id=1, source_target_pairs={{0,24},{1,25},{2,26},{3,27},{4,28},{5,29},{6,30},{7,31}} | collective-permute-start | bytes 294920 | tf_op jit(solution)/shard_map/ppermute | solution.py:17
  37.4 6.8 %collective-permute-start.1 = (bf16[16,3072]{1,0:T(8,128)(2,1)S(1)}, bf16[16,3072]{1,0:T(8,128)(2,1)S(1)}, u32[]{:S(2)}, u32[]{:S(2)}) collective-permute-start(bf16[16,3072]{1,0:T(8,128)(2,1)S(1)} %get-tuple-element.192), channel_id=1, source_target_pairs={{0,16},{8,24},{1,17},{9,25},{2,18},{10,26},{3,19},{11,27},{4,20},{... | collective-permute-start | bytes 294920 | tf_op jit(solution)/shard_map/ppermute | solution.py:17
  38.7 5.6 %collective-permute-start.2 = (bf16[16,3072]{1,0:T(8,128)(2,1)S(1)}, bf16[16,3072]{1,0:T(8,128)(2,1)S(1)}, u32[]{:S(2)}, u32[]{:S(2)}) collective-permute-start(bf16[16,3072]{1,0:T(8,128)(2,1)S(1)} %get-tuple-element.191), channel_id=1, source_target_pairs={{0,8},{8,16},{16,24},{1,9},{9,17},{17,25},{2,10},{10,18},{18,26},{... | collective-permute-start | bytes 294920 | tf_op jit(solution)/shard_map/ppermute | solution.py:17
  40.8 10.8 %all-to-all-start.3 = ((bf16[2,32,3072]{2,1,0:T(8,128)(2,1)}), bf16[2,32,3072]{2,1,0:T(8,128)(2,1)S(1)}, u32[]{:S(2)}, u32[]{:S(2)}) async-start(bf16[2,32,3072]{2,1,0:T(8,128)(2,1)} %bitcast.11), calls=%async_computation.3 | async-start | bytes 786432 | tf_op jit(solution)/shard_map/all_to_all | solution.py:138
